TPU v7x, 256 devices: a whole 4x4x8 slice. The times are simulated.
256 devices in a mesh: seq: 32 (over x_hi, z, core), ch: 8 (over y, x_lo).
Axes of the slice: x: 4 (x_hi: 2, x_lo: 2; x = x_hi * 2 + x_lo), y: 4, z: 8, core: 2. Of those that a mesh axis runs over, the one named last changes fastest.
Arguments:
- hidden: bfloat16 [4096, 2048], P('seq', 'ch'), may hold values from -400 to 400, as said below
- tokens: int32 [4096], replicated, may hold values from 0 to 3
- edit_bounds: int32 [8, 2], replicated, may hold values from 0 to 4095
- norm_gain: float32 [2048], replicated, may hold values from 0.1 to 1.9
- base_embed: float32 [4, 2048], replicated, may hold values from -6 to 6
- w_in: bfloat16 [2, 2048, 4096], P(None, None, 'ch'), may hold values from -0.125 to 0.125
- conv_w: float32 [4, 4096], P(None, 'ch'), may hold values from -3 to 3
- conv_b: float32 [4096], P('ch'), may hold values from -3 to 3
- proj_bc: bfloat16 [32, 4096], P(None, 'ch'), may hold values from -0.1875 to 0.1875
- decay_rate: float32 [16, 4096], P(None, 'ch'), may hold values from 9.765625e-06 to 0.11, as said below
- skip_gain: float32 [4096], P('ch'), may hold values from -4 to 4
- w_out: bfloat16 [4096, 2048], P('ch'), may hold values from -0.09375 to 0.09375
Outputs:
- mixed: bfloat16 [4096, 2048], P('seq', 'ch')
Inputs may be any that keep to these rules, and one draw needn't show every extreme that they name: The hidden states have row and column scales that differ. `decay_rate`: each entry is a positive decay rate per position. `edit_bounds`: positions in the window; a span's start and end come in no fixed order and may coincide with others.
All inputs are finite; a program needn't handle non-finite values.
Results may differ from a plain program's by a relative error of at most 0.014.
Values may be sent and summed in bfloat16 or wider, within the bound.
A program may use at most 64 MiB of HBM per device.

v0:
```python
import jax
import jax.numpy as jnp
from jax import lax
from jax.sharding import PartitionSpec as P

CONV = 4
epsilon = 1e-05


def from_partner(block, axis, apart):
    count = lax.axis_size(axis)
    route = []
    for low in range(count):
        high = low | 1 << apart
        if high != low and high < count:
            route += [(low, high), (high, low)]
    return lax.ppermute(block, axis, route)


def passed_along(block, axis, distance):
    devices = range(lax.axis_size(axis))
    route = [(i - distance, i) for i in devices if i - distance in devices]
    return lax.ppermute(block, axis, route)


def carried_in(part, axis, combine, identity):
    place = lax.axis_index(axis)
    gathered = jax.tree.map(lambda a: lax.all_gather(a, axis), part)
    state = jax.tree.map(lambda a, e: jnp.zeros_like(a) + jnp.asarray(e, a.dtype), part, identity)

    def one(step, state):
        return combine(
            state, jax.tree.map(lambda a: lax.dynamic_index_in_dim(a, step, 0, False), gathered)
        )

    return lax.fori_loop(0, place, one, state)


def link(before, follow):
    return (before[0] * follow[0], before[1] * follow[0] + follow[1])


def link_pair(before, follow):
    return link(before[0:2], follow[0:2]) + link(before[2:4], follow[2:4])


def keep_rows(places, edit_bounds):
    hit_count = jnp.sum(
        (places[:, None] == edit_bounds.reshape(-1)[None, :]).astype(jnp.float32), axis=1
    )
    return 1.0 / (1.0 + hit_count)


def norm_rows(rows, bases, norm_gain, base_embed):
    row_values = rows.astype(jnp.float32)
    inv_rms = lax.rsqrt(jnp.mean(row_values * row_values, axis=1, keepdims=True) + epsilon)
    one_hot = (bases[:, None] == jnp.arange(4, dtype=jnp.int32)[None, :]).astype(jnp.float32)
    embedded = one_hot[:, 0:1] * base_embed[0][None, :]
    for base_index in range(1, 4):
        embedded = (
            embedded + one_hot[:, base_index : base_index + 1] * base_embed[base_index][None, :]
        )
    return (row_values * inv_rms * norm_gain[None, :] + embedded).astype(jnp.bfloat16)


def run_chain(
    start_state, keep_both, inputs_b, inputs_r, mixed_both, decay_mult, drive_gain, want_rows
):
    row_count = mixed_both.shape[1]
    inner_width = mixed_both.shape[2]
    state_size = inputs_b.shape[1]
    turns = 8
    per_turn = row_count // turns
    keep_blocks = keep_both.T.reshape(turns, per_turn, 2)
    b_blocks = inputs_b.transpose(2, 0, 1).reshape(turns, per_turn, 2, state_size)
    r_blocks = inputs_r.transpose(2, 0, 1).reshape(turns, per_turn, 2, state_size)
    x_blocks = mixed_both.transpose(1, 0, 2).reshape(turns, per_turn, 2, inner_width)

    def turn_step(state, block):
        keep_block, b_block, r_block, x_block = block
        outputs = []
        for row_index in range(per_turn):
            x_float = x_block[row_index].astype(jnp.float32)
            state = (
                keep_block[row_index][:, None, None] * decay_mult[None] * state
                + drive_gain[None] * b_block[row_index][:, :, None] * x_float[:, None, :]
            )
            if want_rows:
                outputs.append(jnp.sum(r_block[row_index][:, :, None] * state, axis=1))
        if want_rows:
            return (state, jnp.stack(outputs))
        return (state, jnp.zeros((), jnp.float32))

    final_state, produced = lax.scan(
        turn_step, start_state, (keep_blocks, b_blocks, r_blocks, x_blocks)
    )
    if want_rows:
        return (final_state, produced.reshape(row_count, 2, inner_width).transpose(1, 0, 2))
    return (final_state, None)


def body(
    hidden,
    tokens,
    edit_bounds,
    norm_gain,
    base_embed,
    w_in,
    conv_w,
    conv_b,
    proj_bc,
    decay_rate,
    skip_gain,
    w_out,
):
    row_count = hidden.shape[0]
    seq_count = lax.axis_size("seq")
    where_am = lax.axis_index("seq")
    levels = seq_count.bit_length() - 1
    own_bases = lax.dynamic_slice_in_dim(tokens, where_am * row_count, row_count)
    partner_shard = hidden
    for bit_index in range(levels):
        partner_shard = from_partner(partner_shard, "seq", bit_index)
    owner_dev = seq_count - 1 - where_am
    to_gather = jnp.stack([hidden, partner_shard])
    gathered = lax.all_gather(to_gather, "ch", axis=2, tiled=True)
    normed = norm_rows(gathered[0], own_bases, norm_gain, base_embed)
    far_bases = lax.dynamic_slice_in_dim(tokens, owner_dev * row_count, row_count)
    partner = norm_rows(gathered[1], far_bases, norm_gain, base_embed)
    offsets = jnp.arange(row_count, dtype=jnp.int32)
    keep_ahead = keep_rows(where_am * row_count + offsets, edit_bounds)
    back_rows = partner[::-1, ::-1]
    keep_back = keep_rows(owner_dev * row_count + row_count - 1 - offsets, edit_bounds)
    stacked = jnp.concatenate([normed, back_rows], axis=0)
    both_proj = lax.dot_general(
        stacked, w_in, (((1,), (1,)), ((), ())), preferred_element_type=jnp.float32
    ).astype(jnp.bfloat16)
    x_part = both_proj[:, 0, :].reshape(2, row_count, -1)
    z_part = both_proj[:, 1, :].reshape(2, row_count, -1)
    rims = x_part[:, row_count - CONV + 1 :, :]
    rims_in = passed_along(rims, "seq", 1)
    padded = jnp.concatenate([rims_in, x_part], axis=1)
    conv_sum = conv_b[None, None, :] + jnp.zeros(x_part.shape, jnp.float32)
    for tap_index in range(CONV):
        conv_sum = (
            conv_sum
            + padded[:, tap_index : tap_index + row_count, :].astype(jnp.float32)
            * conv_w[tap_index][None, None, :]
        )
    mixed_in = jax.nn.silu(conv_sum).astype(jnp.bfloat16)
    partial_bc = jnp.einsum("kc,slc->skl", proj_bc, mixed_in, preferred_element_type=jnp.float32)
    inputs_bc = lax.psum(partial_bc, "ch")
    state_size = decay_rate.shape[0]
    inputs_b = inputs_bc[:, :state_size]
    inputs_r = inputs_bc[:, state_size:]
    decay_mult = jnp.exp(-decay_rate)
    drive_gain = jnp.sqrt(-jnp.expm1(-2.0 * decay_rate))
    keep_both = jnp.stack([keep_ahead, keep_back])
    zero_state = jnp.zeros((2,) + decay_rate.shape, jnp.float32)
    local_end, unused = run_chain(
        zero_state, keep_both, inputs_b, inputs_r, mixed_in, decay_mult, drive_gain, False
    )
    block_decay = jnp.exp(-float(row_count) * decay_rate)
    pass_ahead = jnp.prod(keep_ahead) * block_decay
    pass_back = jnp.prod(keep_back) * block_decay
    identity_pair = (jnp.ones_like(decay_mult), jnp.zeros_like(decay_mult))
    carried = carried_in(
        (pass_ahead, local_end[0], pass_back, local_end[1]),
        "seq",
        link_pair,
        identity_pair + identity_pair,
    )
    carry_fore = carried[1]
    carry_aft = carried[3]
    entering = jnp.stack([carry_fore, carry_aft])
    final_unused, read_rows = run_chain(
        entering, keep_both, inputs_b, inputs_r, mixed_in, decay_mult, drive_gain, True
    )
    y_out = read_rows + skip_gain[None, None, :] * mixed_in.astype(jnp.float32)
    gated = (y_out * jax.nn.silu(z_part.astype(jnp.float32))).astype(jnp.bfloat16)
    gated_ahead = gated[0]
    gated_back = gated[1]
    for bit_index in range(levels):
        gated_back = from_partner(gated_back, "seq", bit_index)
    aligned = gated_back[::-1]
    summed = (
        jnp.dot(gated_ahead, w_out, preferred_element_type=jnp.float32)
        + jnp.dot(aligned, w_out, preferred_element_type=jnp.float32)[:, ::-1]
    )
    return lax.psum_scatter(summed.astype(jnp.bfloat16), "ch", scatter_dimension=1, tiled=True)


def solution(mesh):
    placed = (
        P("seq", "ch"),
        P(),
        P(),
        P(),
        P(),
        P(None, None, "ch"),
        P(None, "ch"),
        P("ch"),
        P(None, "ch"),
        P(None, "ch"),
        P("ch"),
        P("ch", None),
    )
    return jax.shard_map(
        body, mesh=mesh, in_specs=placed, out_specs=P("seq", "ch"), check_vma=False
    )
```

profile of v0, /device:TPU:4, one launch (start us, length us, event | category | flops | bytes accessed | tf_op | source)
XLA Modules:
  0.0 528.3 jit_solution(1080955099993510452)
XLA Ops:
  6.5 1.5 collective-permute-done
  8.0 1.9 collective-permute-start.1
  9.9 2.4 collective-permute-done.1
  12.3 3.3 collective-permute-start.2
  15.6 2.6 collective-permute-done.2
  18.2 7.3 %collective-permute-start.3 = (bf16[128,256]{1,0:T(8,128)(2,1)S(1)}, bf16[128,256]{1,0:T(8,128)(2,1)S(1)}, u32[]{:S(2)}, u32[]{:S(2)}) collective-permute-start(bf16[128,256]{1,0:T(8,128)(2,1)S(1)} %collective-permute-done.2), channel_id=1, source_target_pairs={{0,64},{64,0},{8,72},{72,8},{16,80},{80,16},{24,88},{88,24},{32,96... | collective-permute-start | bytes 196616 | tf_op jit(solution)/shard_map/ppermute | solution.py:17
  25.4 2.3 collective-permute-done.3
  27.7 1.5 collective-permute-start.4
  29.2 4.2 collective-permute-done.4
  33.5 1.5 pad_maximum_fusion.1
  36.7 2.6 fusion.187
  40.9 0.9 fusion.196
  41.9 0.9 fusion.198
  42.7 36.3 %all-gather.8.cloned.1.call-done = bf16[2,128,2048]{2,1,0:T(8,128)(2,1)} async-done(((bf16[2,128,256]{2,1,0:T(8,128)(2,1)}), bf16[2,128,2048]{2,1,0:T(8,128)(2,1)}) %all-gather.8.cloned.1.call-update) | async-done | bytes 1048592 | tf_op jit(solution)/shard_map/all_gather | solution.py:126
  79.0 1.5 fusion.168
  80.5 2.9 fusion.171
  83.5 1.8 rev.9
  85.3 3.6 convolution_convert_fusion
  89.0 1.9 collective-permute-start.5
  91.0 6.5 %collective-permute-done.5 = bf16[2,3,512]{2,1,0:T(4,128)(2,1)S(1)} collective-permute-done((bf16[2,3,512]{2,1,0:T(4,128)(2,1)S(1)}, bf16[2,3,512]{2,1,0:T(4,128)(2,1)S(1)}, u32[]{:S(2)}, u32[]{:S(2)}) %collective-permute-start.5) | collective-permute-done | bytes 6176 | tf_op jit(solution)/shard_map/ppermute | solution.py:23
  98.4 34.0 %psum.7 = f32[2,32,128]{2,1,0:T(8,128)S(1)} all-reduce(f32[2,32,128]{2,1,0:T(8,128)S(1)} %convolution_bitcast_fusion), channel_id=1, replica_groups=mesh['seq'=32,'ch'=8] {'ch'}, use_global_device_ids=true, to_apply=%region_5.6 | all-reduce | flops 8192 | bytes 65536 | tf_op jit(solution)/shard_map/psum | solution.py:152
  132.5 5.1 while.41
  139.0 20.7 %all-gather.16.cloned.1.call-done = f32[512,512]{1,0:T(8,128)} async-done(((f32[16,512]{1,0:T(8,128)}), f32[512,512]{1,0:T(8,128)}) %all-gather.16.cloned.1.call-update) | async-done | bytes 1048592 | tf_op jit(solution)/shard_map/all_gather | solution.py:28
  159.7 77.5 %all-gather.14.cloned.1.call-done = f32[512,512]{1,0:T(8,128)} async-done(((f32[16,512]{1,0:T(8,128)}), f32[512,512]{1,0:T(8,128)}) %all-gather.14.cloned.1.call-update) | async-done | bytes 1048592 | tf_op jit(solution)/shard_map/all_gather | solution.py:28
  237.2 77.3 %all-gather.10.cloned.1.call-done = f32[32,16,512]{2,1,0:T(8,128)} async-done(((f32[1,16,512]{2,1,0:T(8,128)}), f32[32,16,512]{2,1,0:T(8,128)}) %all-gather.10.cloned.1.call-update) | async-done | bytes 1048592 | tf_op jit(solution)/shard_map/all_gather | solution.py:28
  314.5 77.3 %all-gather.12.cloned.1.call-done = f32[32,16,512]{2,1,0:T(8,128)} async-done(((f32[1,16,512]{2,1,0:T(8,128)}), f32[32,16,512]{2,1,0:T(8,128)}) %all-gather.12.cloned.1.call-update) | async-done | bytes 1048592 | tf_op jit(solution)/shard_map/all_gather | solution.py:28
  391.8 13.8 %while.39 = (s32[]{:T(128)}, f32[16,512]{1,0:T(8,128)S(1)}, f32[16,512]{1,0:T(8,128)S(1)}, s32[]{:T(128)}, f32[32,16,512]{2,1,0:T(8,128)}, /*index=5*/f32[32,16,...) while((s32[]{:T(128)}, f32[16,512]{1,0:T(8,128)S(1)}, ...), condition=%wide.region_10.11_spmd, body=%wide.region_9.10_spmd.sunk | while | flops 32773 | bytes 262291 | solution.py:36
  392.7 0.8 bitcast_add_fusion.4
  397.0 0.8 bitcast_add_fusion.4
  398.8 0.8 bitcast_add_fusion.4
  400.5 0.8 bitcast_add_fusion.4
  402.2 0.8 bitcast_add_fusion.4
  404.0 0.8 bitcast_add_fusion.4
  405.7 16.8 %while.40 = (s32[]{:T(128)}, f32[2,16,512]{2,1,0:T(8,128)S(1)}, f32[8,16,2,512]{3,2,1,0:T(2,128)}, f32[8,16,2]{2,1,0:T(8,128)S(1)}, f32[16,512]{1,0:T(8,128)S(1)...) while((s32[]{:T(128)}, f32[2,16,512]{2,1,0:T(8,128)S(1)}, ...), condition=%wide.region_28.29_spmd, body=%wide.region_11.28_spmd.sunk | while | flops 2818065 | bytes 1473593 | solution.py:94
  422.5 1.2 fusion.182
  423.7 1.2 collective-permute-start.6
  424.9 1.0 collective-permute-done.6
  425.9 2.6 collective-permute-start.7
  428.5 4.0 collective-permute-done.7
  432.5 6.1 %collective-permute-start.8 = (bf16[128,512]{1,0:T(8,128)(2,1)S(1)}, bf16[128,512]{1,0:T(8,128)(2,1)S(1)}, u32[]{:S(2)}, u32[]{:S(2)}) collective-permute-start(bf16[128,512]{1,0:T(8,128)(2,1)S(1)} %collective-permute-done.7), channel_id=1, source_target_pairs={{0,32},{32,0},{8,40},{40,8},{16,48},{48,16},{24,56},{56,24},{64,96... | collective-permute-start | bytes 393224 | tf_op jit(solution)/shard_map/ppermute | solution.py:17
  438.6 6.3 %collective-permute-done.8 = bf16[128,512]{1,0:T(8,128)(2,1)S(1)} collective-permute-done((bf16[128,512]{1,0:T(8,128)(2,1)S(1)}, bf16[128,512]{1,0:T(8,128)(2,1)S(1)}, u32[]{:S(2)}, u32[]{:S(2)}) %collective-permute-start.8) | collective-permute-done | bytes 131104 | tf_op jit(solution)/shard_map/ppermute | solution.py:17
  444.9 8.6 %collective-permute-start.9 = (bf16[128,512]{1,0:T(8,128)(2,1)S(1)}, bf16[128,512]{1,0:T(8,128)(2,1)S(1)}, u32[]{:S(2)}, u32[]{:S(2)}) collective-permute-start(bf16[128,512]{1,0:T(8,128)(2,1)S(1)} %collective-permute-done.8), channel_id=1, source_target_pairs={{0,64},{64,0},{8,72},{72,8},{16,80},{80,16},{24,88},{88,24},{32,96... | collective-permute-start | bytes 393224 | tf_op jit(solution)/shard_map/ppermute | solution.py:17
  453.5 4.9 collective-permute-done.9
  458.9 6.0 %collective-permute-done.10 = bf16[128,512]{1,0:T(8,128)(2,1)S(1)} collective-permute-done((bf16[128,512]{1,0:T(8,128)(2,1)S(1)}, bf16[128,512]{1,0:T(8,128)(2,1)S(1)}, u32[]{:S(2)}, u32[]{:S(2)}) %collective-permute-start.10) | collective-permute-done | bytes 131104 | tf_op jit(solution)/shard_map/ppermute | solution.py:17
  465.1 1.5 fusion.199
  466.6 9.3 %rev.11 = f32[128,2048]{1,0:T(8,128)} reverse(f32[128,2048]{1,0:T(8,128)} %fusion.199), dimensions={1} | reverse | bytes 2097152 | tf_op jit(solution)/shard_map/rev | solution.py:188
  475.9 2.1 add_convert_fusion
  478.1 43.4 %reduce-scatter.2.cloned.1.call-done = bf16[128,256]{1,0:T(8,128)(2,1)} async-done(((bf16[128,2048]{1,0:T(8,128)(2,1)}), bf16[128,256]{1,0:T(8,128)(2,1)}) %reduce-scatter.2.cloned.1.call-update) | async-done | bytes 65552 | tf_op jit(solution)/shard_map/reduce_scatter | solution.py:190
  (294 shorter events, 35.5 us)
Async XLA Ops:
  6.5 451.9 %copy-start = (bf16[512,2048]{1,0:T(8,128)(2,1)S(1)}, bf16[512,2048]{1,0:T(8,128)(2,1)}, u32[]{:S(2)}) copy-start(bf16[512,2048]{1,0:T(8,128)(2,1)} %param.29) | copy-start | bytes 6291460
  6.5 72.5 %all-gather.8.cloned.1.call-start = ((), (), s32[]{:S(2)}) async-start(), calls=%async_computation.1 | async-start | bytes 1179648 | tf_op jit(solution)/shard_map/all_gather | solution.py:126
  6.5 1.5 collective-permute-start
  8.0 4.3 collective-permute-start.1
  12.3 5.8 %collective-permute-start.2 = (bf16[128,256]{1,0:T(8,128)(2,1)S(1)}, bf16[128,256]{1,0:T(8,128)(2,1)S(1)}, u32[]{:S(2)}, u32[]{:S(2)}) collective-permute-start(bf16[128,256]{1,0:T(8,128)(2,1)S(1)} %collective-permute-done.1), channel_id=1, source_target_pairs={{0,32},{32,0},{8,40},{40,8},{16,48},{48,16},{24,56},{56,24},{64,96... | collective-permute-start | bytes 196616 | tf_op jit(solution)/shard_map/ppermute | solution.py:17
  18.2 9.5 %collective-permute-start.3 = (bf16[128,256]{1,0:T(8,128)(2,1)S(1)}, bf16[128,256]{1,0:T(8,128)(2,1)S(1)}, u32[]{:S(2)}, u32[]{:S(2)}) collective-permute-start(bf16[128,256]{1,0:T(8,128)(2,1)S(1)} %collective-permute-done.2), channel_id=1, source_target_pairs={{0,64},{64,0},{8,72},{72,8},{16,80},{80,16},{24,88},{88,24},{32,96... | collective-permute-start | bytes 196616 | tf_op jit(solution)/shard_map/ppermute | solution.py:17
  27.7 5.8 %collective-permute-start.4 = (bf16[128,256]{1,0:T(8,128)(2,1)S(1)}, bf16[128,256]{1,0:T(8,128)(2,1)S(1)}, u32[]{:S(2)}, u32[]{:S(2)}) collective-permute-start(bf16[128,256]{1,0:T(8,128)(2,1)S(1)} %collective-permute-done.3), channel_id=1, source_target_pairs={{0,128},{128,0},{8,136},{136,8},{16,144},{144,16},{24,152},{152,24... | collective-permute-start | bytes 196616 | tf_op jit(solution)/shard_map/ppermute | solution.py:17
  35.0 124.7 %all-gather.16.cloned.1.call-start = ((), (), s32[]{:S(2)}) async-start(), calls=%async_computation.6 | async-start | bytes 1081344 | tf_op jit(solution)/shard_map/all_gather | solution.py:28
  39.3 197.9 %all-gather.14.cloned.1.call-start = ((), (), s32[]{:S(2)}) async-start(), calls=%async_computation.5 | async-start | bytes 1081344 | tf_op jit(solution)/shard_map/all_gather | solution.py:28
  40.1 274.4 %all-gather.10.cloned.1.call-start = ((), (), s32[]{:S(2)}) async-start(), calls=%async_computation.2 | async-start | bytes 1081344 | tf_op jit(solution)/shard_map/all_gather | solution.py:28
  85.3 12.3 %copy-start.2 = (f32[512]{0:T(512)S(1)}, f32[512]{0:T(512)}, u32[]{:S(2)}) copy-start(f32[512]{0:T(512)} %param.25) | copy-start | bytes 6148
  88.9 9.3 %copy-start.1 = (bf16[32,512]{1,0:T(8,128)(2,1)S(1)}, bf16[32,512]{1,0:T(8,128)(2,1)}, u32[]{:S(2)}) copy-start(bf16[32,512]{1,0:T(8,128)(2,1)} %param.26) | copy-start | bytes 98308
  89.0 8.6 %collective-permute-start.5 = (bf16[2,3,512]{2,1,0:T(4,128)(2,1)S(1)}, bf16[2,3,512]{2,1,0:T(4,128)(2,1)S(1)}, u32[]{:S(2)}, u32[]{:S(2)}) collective-permute-start(bf16[2,3,512]{2,1,0:T(4,128)(2,1)S(1)} %slice.623), channel_id=1, source_target_pairs={{0,8},{8,16},{16,24},{24,32},{32,40},{40,48},{48,56},{56,64},{64,7... | collective-permute-start | bytes 18440 | tf_op jit(solution)/shard_map/ppermute | solution.py:23
  138.3 253.6 %all-gather.12.cloned.1.call-start = ((), (), s32[]{:S(2)}) async-start(), calls=%async_computation.3 | async-start | bytes 1081344 | tf_op jit(solution)/shard_map/all_gather | solution.py:28
  138.9 382.6 %reduce-scatter.2.cloned.1.call-start = ((), (), s32[]{:S(2)}) async-start(), calls=%async_computation.4 | async-start | bytes 589824 | tf_op jit(solution)/shard_map/reduce_scatter | solution.py:190
  405.7 16.8 %copy-start.3 = (f32[512]{0:T(512)S(1)}, f32[512]{0:T(512)}, u32[]{:S(2)}) copy-start(f32[512]{0:T(512)} %param.28) | copy-start | bytes 6148
  423.7 2.2 collective-permute-start.6
  425.9 6.7 %collective-permute-start.7 = (bf16[128,512]{1,0:T(8,128)(2,1)S(1)}, bf16[128,512]{1,0:T(8,128)(2,1)S(1)}, u32[]{:S(2)}, u32[]{:S(2)}) collective-permute-start(bf16[128,512]{1,0:T(8,128)(2,1)S(1)} %collective-permute-done.6), channel_id=1, source_target_pairs={{0,16},{16,0},{8,24},{24,8},{32,48},{48,32},{40,56},{56,40},{64,80... | collective-permute-start | bytes 393224 | tf_op jit(solution)/shard_map/ppermute | solution.py:17
  432.5 12.4 %collective-permute-start.8 = (bf16[128,512]{1,0:T(8,128)(2,1)S(1)}, bf16[128,512]{1,0:T(8,128)(2,1)S(1)}, u32[]{:S(2)}, u32[]{:S(2)}) collective-permute-start(bf16[128,512]{1,0:T(8,128)(2,1)S(1)} %collective-permute-done.7), channel_id=1, source_target_pairs={{0,32},{32,0},{8,40},{40,8},{16,48},{48,16},{24,56},{56,24},{64,96... | collective-permute-start | bytes 393224 | tf_op jit(solution)/shard_map/ppermute | solution.py:17
  444.9 13.5 %collective-permute-start.9 = (bf16[128,512]{1,0:T(8,128)(2,1)S(1)}, bf16[128,512]{1,0:T(8,128)(2,1)S(1)}, u32[]{:S(2)}, u32[]{:S(2)}) collective-permute-start(bf16[128,512]{1,0:T(8,128)(2,1)S(1)} %collective-permute-done.8), channel_id=1, source_target_pairs={{0,64},{64,0},{8,72},{72,8},{16,80},{80,16},{24,88},{88,24},{32,96... | collective-permute-start | bytes 393224 | tf_op jit(solution)/shard_map/ppermute | solution.py:17
  458.4 6.5 %collective-permute-start.10 = (bf16[128,512]{1,0:T(8,128)(2,1)S(1)}, bf16[128,512]{1,0:T(8,128)(2,1)S(1)}, u32[]{:S(2)}, u32[]{:S(2)}) collective-permute-start(bf16[128,512]{1,0:T(8,128)(2,1)S(1)} %collective-permute-done.9), channel_id=1, source_target_pairs={{0,128},{128,0},{8,136},{136,8},{16,144},{144,16},{24,152},{152,24... | collective-permute-start | bytes 393224 | tf_op jit(solution)/shard_map/ppermute | solution.py:17
Sparse Core Ops, SparseCore 0:
  35.1 43.8 all-gather.7
  81.8 77.8 all-gather.15
  162.5 74.6 all-gather.13
  239.8 74.5 all-gather.9
  317.1 74.6 all-gather.11
  478.2 43.2 reduce-scatter.1
where the time goes:
time: 532 us; the launch traced here: 528 us
  waiting for transfers between devices  375 us (70%)
  other arithmetic  38.7 us (7%)
  starting transfers between devices  34.7 us (7%)
  blocking collectives  34 us (6%)
  local copies, waits for them, and re-layouts  24.6 us (5%)
  between operations  13.7 us (3%)
  matrix products  5.68 us (1%)
    all_gather x4, waiting for transfers between devices, carried_in(): gathered = jax.tree.map(lambda a: lax.all_gather(a, axis), part)  253 us
    reduce_scatter x1, waiting for transfers between devices, body(): lax.psum_scatter(summed.astype(jnp.bfloat16), 'ch', scatter_dimension=1,...  43.4 us
    all_gather x1, waiting for transfers between devices, body(): gathered = lax.all_gather(to_gather, 'ch', axis=2, tiled=True)  36.3 us
    ppermute x10, waiting for transfers between devices, from_partner(): return lax.ppermute(block, axis, route)  35.1 us
    psum x1, blocking collectives, body(): inputs_bc = lax.psum(partial_bc, 'ch')  34 us
    ppermute x10, starting transfers between devices, from_partner(): return lax.ppermute(block, axis, route)  32.5 us
    add x16, other arithmetic, link(): return (before[0] * follow[0], before[1] * follow[0] + follow[1])  13.5 us
  transfers between devices with their start and end apart: 17, of which 17 were waited for; matrix products, arithmetic and copies ran while one was open for 4% of the time, Pallas kernels for 0%

commit v1 on v0

--- a/solution.py
+++ b/solution.py
@@ -5,6 +5,18 @@
 
 CONV = 4
 epsilon = 1e-05
+
+
+def expand_columns(local, row_dim):
+    return jnp.concatenate(
+        lax.all_to_all(
+            jnp.stack([local for _ in range(lax.axis_size("ch"))]),
+            axis_name="ch",
+            split_axis=0,
+            concat_axis=0,
+        ),
+        axis=row_dim,
+    )
 
 
 def from_partner(block, axis, apart):
@@ -123,7 +135,7 @@
         partner_shard = from_partner(partner_shard, "seq", bit_index)
     owner_dev = seq_count - 1 - where_am
     to_gather = jnp.stack([hidden, partner_shard])
-    gathered = lax.all_gather(to_gather, "ch", axis=2, tiled=True)
+    gathered = expand_columns(to_gather, 2)
     normed = norm_rows(gathered[0], own_bases, norm_gain, base_embed)
     far_bases = lax.dynamic_slice_in_dim(tokens, owner_dev * row_count, row_count)
     partner = norm_rows(gathered[1], far_bases, norm_gain, base_embed)

time: 532 us -> 462 us (0.87)
  waiting for transfers between devices: 375 us -> 306 us
    all_gather x4, waiting for transfers between devices: 253 us -> 209 us  [carried_in(): gathered = jax.tree.map(lambda a: lax.all_gather(a, axis), part)]
    all_gather x1 -> x0, waiting for transfers between devices: 36.3 us -> none  [body(): gathered = lax.all_gather(to_gather, 'ch', axis=2, tiled=True)]
    all_to_all x0 -> x1, waiting for transfers between devices: none -> 12.2 us  [expand_columns(): lax.all_to_all(jnp.stack([local for _ in range(lax.axis_size('ch'))]), ax...]
  transfers between devices with their start and end apart: 17 -> 17, of which waited for: 17 -> 16; matrix products, arithmetic and copies ran while one was open for 4% -> 4% of each run, Pallas kernels for 0% -> 0%
where the time goes in v1:
time: 462 us; the launch traced here: 459 us
  waiting for transfers between devices  306 us (66%)
  starting transfers between devices  39.9 us (9%)
  other arithmetic  35.9 us (8%)
  blocking collectives  31.5 us (7%)
  local copies, waits for them, and re-layouts  24.8 us (5%)
  between operations  13.4 us (3%)
  matrix products  5.79 us (1%)
    all_gather x4, waiting for transfers between devices, carried_in(): gathered = jax.tree.map(lambda a: lax.all_gather(a, axis), part)  209 us
    reduce_scatter x1, waiting for transfers between devices, body(): lax.psum_scatter(summed.astype(jnp.bfloat16), 'ch', scatter_dimension=1,...  43.4 us
    ppermute x10, waiting for transfers between devices, from_partner(): return lax.ppermute(block, axis, route)  34.3 us
    ppermute x10, starting transfers between devices, from_partner(): return lax.ppermute(block, axis, route)  32.7 us
    psum x1, blocking collectives, body(): inputs_bc = lax.psum(partial_bc, 'ch')  31.5 us
    add x16, other arithmetic, link(): return (before[0] * follow[0], before[1] * follow[0] + follow[1])  13.5 us
    all_to_all x1, waiting for transfers between devices, expand_columns(): lax.all_to_all(jnp.stack([local for _ in range(lax.axis_size('ch'))]), ax...  12.2 us
    rev x1, local copies, waits for them, and re-layouts, body(): jnp.dot(aligned, w_out, preferred_element_type=jnp.float32)[:, ::-1]  9.34 us
  transfers between devices with their start and end apart: 17, of which 16 were waited for; matrix products, arithmetic and copies ran while one was open for 4% of the time, Pallas kernels for 0%

profile of v1, /device:TPU:4, one launch (start us, length us, event | category | flops | bytes accessed | tf_op | source)
XLA Modules:
  0.0 458.5 jit_solution(10507194416049495411)
XLA Ops:
  6.6 0.9 copy.39
  8.4 2.6 fusion.179
  11.2 1.4 collective-permute-done
  12.6 1.9 collective-permute-start.1
  14.5 2.4 collective-permute-done.1
  16.9 3.3 collective-permute-start.2
  20.2 2.5 collective-permute-done.2
  22.8 7.3 %collective-permute-start.3 = (bf16[128,256]{1,0:T(8,128)(2,1)S(1)}, bf16[128,256]{1,0:T(8,128)(2,1)S(1)}, u32[]{:S(2)}, u32[]{:S(2)}) collective-permute-start(bf16[128,256]{1,0:T(8,128)(2,1)S(1)} %collective-permute-done.2), channel_id=1, source_target_pairs={{0,64},{64,0},{8,72},{72,8},{16,80},{80,16},{24,88},{88,24},{32,96... | collective-permute-start | bytes 196616 | tf_op jit(solution)/shard_map/ppermute | solution.py:29
  30.8 1.5 collective-permute-done.3
  32.3 1.6 collective-permute-start.4
  33.9 4.2 collective-permute-done.4
  38.1 0.9 pad_maximum_fusion.1
  39.0 1.1 stack.89
  40.0 5.1 %all-to-all-start = ((bf16[8,2,128,256]{3,2,1,0:T(8,128)(2,1)}), bf16[8,2,128,256]{3,2,1,0:T(8,128)(2,1)S(1)}, u32[]{:S(2)}, u32[]{:S(2)}) async-start(bf16[8,2,128,256]{3,2,1,0:T(8,128)(2,1)} %stack.89), calls=%async_computation | async-start | bytes 2097152 | tf_op jit(solution)/shard_map/all_to_all | solution.py:12
  45.3 12.2 %all-to-all-done = bf16[8,2,128,256]{3,2,1,0:T(8,128)(2,1)S(1)} async-done(((bf16[8,2,128,256]{3,2,1,0:T(8,128)(2,1)}), bf16[8,2,128,256]{3,2,1,0:T(8,128)(2,1)S(1)}, u32[]{:S(2)}, u32[]{:S(2)}) %all-to-all-start) | async-done | bytes 1048608 | tf_op jit(solution)/shard_map/all_to_all | solution.py:12
  58.7 1.7 add_convert_fusion.2
  60.4 1.8 rev.9
  62.2 3.7 convolution_convert_fusion
  66.0 1.9 collective-permute-start.5
  68.0 6.5 %collective-permute-done.5 = bf16[2,3,512]{2,1,0:T(4,128)(2,1)S(1)} collective-permute-done((bf16[2,3,512]{2,1,0:T(4,128)(2,1)S(1)}, bf16[2,3,512]{2,1,0:T(4,128)(2,1)S(1)}, u32[]{:S(2)}, u32[]{:S(2)}) %collective-permute-start.5) | collective-permute-done | bytes 6176 | tf_op jit(solution)/shard_map/ppermute | solution.py:35
  75.4 31.5 %psum.7 = f32[2,32,128]{2,1,0:T(8,128)S(1)} all-reduce(f32[2,32,128]{2,1,0:T(8,128)S(1)} %convolution_bitcast_fusion), channel_id=1, replica_groups=mesh['seq'=32,'ch'=8] {'ch'}, use_global_device_ids=true, to_apply=%region_5.6 | all-reduce | flops 8192 | bytes 65536 | tf_op jit(solution)/shard_map/psum | solution.py:164
  107.1 5.1 %while.41 = (s32[]{:T(128)}, f32[2,16,512]{2,1,0:T(8,128)S(1)}, f32[8,16,2]{2,1,0:T(8,128)S(1)}, f32[16,512]{1,0:T(8,128)S(1)}, f32[16,512]{1,0:T(8,128)S(1)}, /...) while((s32[]{:T(128)}, f32[2,16,512]{2,1,0:T(8,128)S(1)}, ...), condition=%wide.region_7.8_spmd.clone, body=%wide.region_6.7_spmd.clone.sunk | while | flops 1343506 | bytes 367571 | solution.py:106
  113.6 53.9 %all-gather.11.cloned.1.call-done = f32[512,512]{1,0:T(8,128)} async-done(((f32[16,512]{1,0:T(8,128)}), f32[512,512]{1,0:T(8,128)}) %all-gather.11.cloned.1.call-update) | async-done | bytes 1048592 | tf_op jit(solution)/shard_map/all_gather | solution.py:40
  167.5 77.4 %all-gather.7.cloned.1.call-done = f32[32,16,512]{2,1,0:T(8,128)} async-done(((f32[1,16,512]{2,1,0:T(8,128)}), f32[32,16,512]{2,1,0:T(8,128)}) %all-gather.7.cloned.1.call-update) | async-done | bytes 1048592 | tf_op jit(solution)/shard_map/all_gather | solution.py:40
  245.0 77.4 %all-gather.9.cloned.1.call-done = f32[32,16,512]{2,1,0:T(8,128)} async-done(((f32[1,16,512]{2,1,0:T(8,128)}), f32[32,16,512]{2,1,0:T(8,128)}) %all-gather.9.cloned.1.call-update) | async-done | bytes 1048592 | tf_op jit(solution)/shard_map/all_gather | solution.py:40
  322.3 13.8 %while.39 = (s32[]{:T(128)}, f32[16,512]{1,0:T(8,128)S(1)}, f32[16,512]{1,0:T(8,128)S(1)}, s32[]{:T(128)}, f32[32,16,512]{2,1,0:T(8,128)}, /*index=5*/f32[32,16,...) while((s32[]{:T(128)}, f32[16,512]{1,0:T(8,128)S(1)}, ...), condition=%wide.region_10.11_spmd, body=%wide.region_9.10_spmd.sunk | while | flops 32773 | bytes 262291 | solution.py:48
  323.2 0.8 bitcast_add_fusion.4
  324.1 0.8 bitcast_add_fusion.4
  325.8 0.8 bitcast_add_fusion.4
  327.5 0.8 bitcast_add_fusion.4
  329.2 0.8 bitcast_add_fusion.4
  331.0 0.8 bitcast_add_fusion.4
  332.7 0.8 bitcast_add_fusion.4
  336.2 16.8 %while.40 = (s32[]{:T(128)}, f32[2,16,512]{2,1,0:T(8,128)S(1)}, f32[8,16,2,512]{3,2,1,0:T(2,128)}, f32[8,16,2]{2,1,0:T(8,128)S(1)}, f32[16,512]{1,0:T(8,128)S(1)...) while((s32[]{:T(128)}, f32[2,16,512]{2,1,0:T(8,128)S(1)}, ...), condition=%wide.region_28.29_spmd, body=%wide.region_11.28_spmd.sunk | while | flops 2818065 | bytes 1473593 | solution.py:106
  352.9 1.2 fusion.174
  354.2 1.2 collective-permute-start.6
  355.4 1.0 collective-permute-done.6
  356.4 2.6 collective-permute-start.7
  359.0 4.0 collective-permute-done.7
  363.0 6.1 %collective-permute-start.8 = (bf16[128,512]{1,0:T(8,128)(2,1)S(1)}, bf16[128,512]{1,0:T(8,128)(2,1)S(1)}, u32[]{:S(2)}, u32[]{:S(2)}) collective-permute-start(bf16[128,512]{1,0:T(8,128)(2,1)S(1)} %collective-permute-done.7), channel_id=1, source_target_pairs={{0,32},{32,0},{8,40},{40,8},{16,48},{48,16},{24,56},{56,24},{64,96... | collective-permute-start | bytes 393224 | tf_op jit(solution)/shard_map/ppermute | solution.py:29
  369.1 6.3 %collective-permute-done.8 = bf16[128,512]{1,0:T(8,128)(2,1)S(1)} collective-permute-done((bf16[128,512]{1,0:T(8,128)(2,1)S(1)}, bf16[128,512]{1,0:T(8,128)(2,1)S(1)}, u32[]{:S(2)}, u32[]{:S(2)}) %collective-permute-start.8) | collective-permute-done | bytes 131104 | tf_op jit(solution)/shard_map/ppermute | solution.py:29
  375.4 8.6 %collective-permute-start.9 = (bf16[128,512]{1,0:T(8,128)(2,1)S(1)}, bf16[128,512]{1,0:T(8,128)(2,1)S(1)}, u32[]{:S(2)}, u32[]{:S(2)}) collective-permute-start(bf16[128,512]{1,0:T(8,128)(2,1)S(1)} %collective-permute-done.8), channel_id=1, source_target_pairs={{0,64},{64,0},{8,72},{72,8},{16,80},{80,16},{24,88},{88,24},{32,96... | collective-permute-start | bytes 393224 | tf_op jit(solution)/shard_map/ppermute | solution.py:29
  384.0 4.9 %collective-permute-done.9 = bf16[128,512]{1,0:T(8,128)(2,1)S(1)} collective-permute-done((bf16[128,512]{1,0:T(8,128)(2,1)S(1)}, bf16[128,512]{1,0:T(8,128)(2,1)S(1)}, u32[]{:S(2)}, u32[]{:S(2)}) %collective-permute-start.9) | collective-permute-done | bytes 131104 | tf_op jit(solution)/shard_map/ppermute | solution.py:29
  389.4 6.0 %collective-permute-done.10 = bf16[128,512]{1,0:T(8,128)(2,1)S(1)} collective-permute-done((bf16[128,512]{1,0:T(8,128)(2,1)S(1)}, bf16[128,512]{1,0:T(8,128)(2,1)S(1)}, u32[]{:S(2)}, u32[]{:S(2)}) %collective-permute-start.10) | collective-permute-done | bytes 131104 | tf_op jit(solution)/shard_map/ppermute | solution.py:29
  395.6 1.5 fusion.191
  397.0 9.3 %rev.11 = f32[128,2048]{1,0:T(8,128)} reverse(f32[128,2048]{1,0:T(8,128)} %fusion.191), dimensions={1} | reverse | bytes 2097152 | tf_op jit(solution)/shard_map/rev | solution.py:200
  406.4 2.1 add_convert_fusion
  408.6 43.4 %reduce-scatter.2.cloned.1.call-done = bf16[128,256]{1,0:T(8,128)(2,1)} async-done(((bf16[128,2048]{1,0:T(8,128)(2,1)}), bf16[128,256]{1,0:T(8,128)(2,1)}) %reduce-scatter.2.cloned.1.call-update) | async-done | bytes 65552 | tf_op jit(solution)/shard_map/reduce_scatter | solution.py:202
  (303 shorter events, 34.5 us)
Async XLA Ops:
  6.5 382.4 %copy-start = (bf16[512,2048]{1,0:T(8,128)(2,1)S(1)}, bf16[512,2048]{1,0:T(8,128)(2,1)}, u32[]{:S(2)}) copy-start(bf16[512,2048]{1,0:T(8,128)(2,1)} %param.29) | copy-start | bytes 6291460
  6.5 38.7 %copy-start.4 = (f32[4,512]{1,0:T(4,128)S(1)}, f32[4,512]{1,0:T(4,128)}, u32[]{:S(2)}) copy-start(f32[4,512]{1,0:T(4,128)} %param.24) | copy-start | bytes 24580
  6.5 38.7 %copy-start.2 = (f32[4,2048]{1,0:T(4,128)S(1)}, f32[4,2048]{1,0:T(4,128)}, u32[]{:S(2)}) copy-start(f32[4,2048]{1,0:T(4,128)} %param.22) | copy-start | bytes 98308
  6.5 107.1 %all-gather.13.cloned.1.call-start = ((), (), s32[]{:S(2)}) async-start(), calls=%async_computation.6 | async-start | bytes 1081344 | tf_op jit(solution)/shard_map/all_gather | solution.py:40
  11.0 156.5 %all-gather.11.cloned.1.call-start = ((), (), s32[]{:S(2)}) async-start(), calls=%async_computation.5 | async-start | bytes 1081344 | tf_op jit(solution)/shard_map/all_gather | solution.py:40
  11.1 1.6 collective-permute-start
  12.6 4.3 collective-permute-start.1
  16.9 5.8 %collective-permute-start.2 = (bf16[128,256]{1,0:T(8,128)(2,1)S(1)}, bf16[128,256]{1,0:T(8,128)(2,1)S(1)}, u32[]{:S(2)}, u32[]{:S(2)}) collective-permute-start(bf16[128,256]{1,0:T(8,128)(2,1)S(1)} %collective-permute-done.1), channel_id=1, source_target_pairs={{0,32},{32,0},{8,40},{40,8},{16,48},{48,16},{24,56},{56,24},{64,96... | collective-permute-start | bytes 196616 | tf_op jit(solution)/shard_map/ppermute | solution.py:29
  22.8 9.6 %collective-permute-start.3 = (bf16[128,256]{1,0:T(8,128)(2,1)S(1)}, bf16[128,256]{1,0:T(8,128)(2,1)S(1)}, u32[]{:S(2)}, u32[]{:S(2)}) collective-permute-start(bf16[128,256]{1,0:T(8,128)(2,1)S(1)} %collective-permute-done.2), channel_id=1, source_target_pairs={{0,64},{64,0},{8,72},{72,8},{16,80},{80,16},{24,88},{88,24},{32,96... | collective-permute-start | bytes 196616 | tf_op jit(solution)/shard_map/ppermute | solution.py:29
  32.3 5.8 %collective-permute-start.4 = (bf16[128,256]{1,0:T(8,128)(2,1)S(1)}, bf16[128,256]{1,0:T(8,128)(2,1)S(1)}, u32[]{:S(2)}, u32[]{:S(2)}) collective-permute-start(bf16[128,256]{1,0:T(8,128)(2,1)S(1)} %collective-permute-done.3), channel_id=1, source_target_pairs={{0,128},{128,0},{8,136},{136,8},{16,144},{144,16},{24,152},{152,24... | collective-permute-start | bytes 196616 | tf_op jit(solution)/shard_map/ppermute | solution.py:29
  40.0 17.4 %all-to-all-start = ((bf16[8,2,128,256]{3,2,1,0:T(8,128)(2,1)}), bf16[8,2,128,256]{3,2,1,0:T(8,128)(2,1)S(1)}, u32[]{:S(2)}, u32[]{:S(2)}) async-start(bf16[8,2,128,256]{3,2,1,0:T(8,128)(2,1)} %stack.89), calls=%async_computation | async-start | bytes 2097152 | tf_op jit(solution)/shard_map/all_to_all | solution.py:12
  45.2 199.8 %all-gather.7.cloned.1.call-start = ((), (), s32[]{:S(2)}) async-start(), calls=%async_computation.2 | async-start | bytes 1081344 | tf_op jit(solution)/shard_map/all_gather | solution.py:40
  58.0 0.7 copy-start.3
  62.2 12.4 %copy-start.5 = (f32[512]{0:T(512)S(1)}, f32[512]{0:T(512)}, u32[]{:S(2)}) copy-start(f32[512]{0:T(512)} %param.25) | copy-start | bytes 6148
  65.9 9.3 %copy-start.1 = (bf16[32,512]{1,0:T(8,128)(2,1)S(1)}, bf16[32,512]{1,0:T(8,128)(2,1)}, u32[]{:S(2)}) copy-start(bf16[32,512]{1,0:T(8,128)(2,1)} %param.26) | copy-start | bytes 98308
  66.0 8.6 %collective-permute-start.5 = (bf16[2,3,512]{2,1,0:T(4,128)(2,1)S(1)}, bf16[2,3,512]{2,1,0:T(4,128)(2,1)S(1)}, u32[]{:S(2)}, u32[]{:S(2)}) collective-permute-start(bf16[2,3,512]{2,1,0:T(4,128)(2,1)S(1)} %slice.625), channel_id=1, source_target_pairs={{0,8},{8,16},{16,24},{24,32},{32,40},{40,48},{48,56},{56,64},{64,7... | collective-permute-start | bytes 18440 | tf_op jit(solution)/shard_map/ppermute | solution.py:35
  112.8 209.5 %all-gather.9.cloned.1.call-start = ((), (), s32[]{:S(2)}) async-start(), calls=%async_computation.3 | async-start | bytes 1081344 | tf_op jit(solution)/shard_map/all_gather | solution.py:40
  113.4 338.5 %reduce-scatter.2.cloned.1.call-start = ((), (), s32[]{:S(2)}) async-start(), calls=%async_computation.4 | async-start | bytes 589824 | tf_op jit(solution)/shard_map/reduce_scatter | solution.py:202
  336.2 16.8 %copy-start.6 = (f32[512]{0:T(512)S(1)}, f32[512]{0:T(512)}, u32[]{:S(2)}) copy-start(f32[512]{0:T(512)} %param.28) | copy-start | bytes 6148
  354.2 2.2 collective-permute-start.6
  356.4 6.7 %collective-permute-start.7 = (bf16[128,512]{1,0:T(8,128)(2,1)S(1)}, bf16[128,512]{1,0:T(8,128)(2,1)S(1)}, u32[]{:S(2)}, u32[]{:S(2)}) collective-permute-start(bf16[128,512]{1,0:T(8,128)(2,1)S(1)} %collective-permute-done.6), channel_id=1, source_target_pairs={{0,16},{16,0},{8,24},{24,8},{32,48},{48,32},{40,56},{56,40},{64,80... | collective-permute-start | bytes 393224 | tf_op jit(solution)/shard_map/ppermute | solution.py:29
  363.0 12.4 %collective-permute-start.8 = (bf16[128,512]{1,0:T(8,128)(2,1)S(1)}, bf16[128,512]{1,0:T(8,128)(2,1)S(1)}, u32[]{:S(2)}, u32[]{:S(2)}) collective-permute-start(bf16[128,512]{1,0:T(8,128)(2,1)S(1)} %collective-permute-done.7), channel_id=1, source_target_pairs={{0,32},{32,0},{8,40},{40,8},{16,48},{48,16},{24,56},{56,24},{64,96... | collective-permute-start | bytes 393224 | tf_op jit(solution)/shard_map/ppermute | solution.py:29
  375.4 13.5 %collective-permute-start.9 = (bf16[128,512]{1,0:T(8,128)(2,1)S(1)}, bf16[128,512]{1,0:T(8,128)(2,1)S(1)}, u32[]{:S(2)}, u32[]{:S(2)}) collective-permute-start(bf16[128,512]{1,0:T(8,128)(2,1)S(1)} %collective-permute-done.8), channel_id=1, source_target_pairs={{0,64},{64,0},{8,72},{72,8},{16,80},{80,16},{24,88},{88,24},{32,96... | collective-permute-start | bytes 393224 | tf_op jit(solution)/shard_map/ppermute | solution.py:29
  388.9 6.5 %collective-permute-start.10 = (bf16[128,512]{1,0:T(8,128)(2,1)S(1)}, bf16[128,512]{1,0:T(8,128)(2,1)S(1)}, u32[]{:S(2)}, u32[]{:S(2)}) collective-permute-start(bf16[128,512]{1,0:T(8,128)(2,1)S(1)} %collective-permute-done.9), channel_id=1, source_target_pairs={{0,128},{128,0},{8,136},{136,8},{16,144},{144,16},{24,152},{152,24... | collective-permute-start | bytes 393224 | tf_op jit(solution)/shard_map/ppermute | solution.py:29
Sparse Core Ops, SparseCore 0:
  11.1 78.9 all-gather.12
  92.9 74.6 all-gather.10
  170.3 74.5 all-gather.6
  247.6 74.6 all-gather.8
  408.7 43.2 reduce-scatter.1
